TPU v7x, 512 devices: a whole 4x4x16 slice. The times are simulated.
512 devices in a mesh: space: 32 (over z_lo, x, core), species: 16 (over y, z_hi).
Axes of the slice: x: 4, y: 4, z: 16 (z_hi: 4, z_lo: 4; z = z_hi * 4 + z_lo), core: 2. Of those that a mesh axis runs over, the one named last changes fastest.
Arguments:
- biomass: bfloat16 [512, 64, 1024], P('species', 'space'), may hold values from 0.019897461 to 1
- resources: float32 [128, 64, 1024], P('species', 'space'), may hold values from 0.1 to 4
- capacity: float32 [512, 128], P('species'), may hold values from 0.002 to 0.05
- affinity: float32 [512, 128], P('species'), may hold values from 0.2 to 5
- secretion: bfloat16 [128, 512], P(None, 'species'), may hold values from 0 to 0.059814453
- energy_yield: float32 [128], replicated, may hold values from 0.5 to 2
- maintenance: float32 [512], P('species'), may hold values from 0.3 to 3
- motility: float32 [512], P('species'), may hold values from 0.04 to 0.6
- diffusivity: float32 [128], P('species'), may hold values from 0.02 to 0.6
- supply: float32 [128], P('species'), may hold values from 0.4 to 4
Outputs:
- growth: float32 [512, 64, 1024], P('species', 'space')
- new_biomass: float32 [512, 64, 1024], P('species', 'space')
- new_resources: float32 [128, 64, 1024], P('species', 'space')
All inputs are finite; a program needn't handle non-finite values.
Results may differ from a plain program's by a relative error of at most 0.0003.
Values may be sent and summed in bfloat16 or wider, within the bound.
A program may use at most 64 MiB of HBM per device.

v0:
```python
import math

import jax
import jax.numpy as jnp
from jax import lax
from jax.sharding import PartitionSpec as P

NY = 16
NZ = 64


time_step = 0.25


def extended_2(block, sides, width):
    for axis, dim in sides:
        count = lax.axis_size(axis)
        forward = [(i, i + 1) for i in range(count - 1)]
        forward.append((count - 1, 0))
        backward = [(target, source) for source, target in forward]
        low = lax.ppermute(
            lax.slice_in_dim(block, block.shape[dim] - width, None, axis=dim), axis, forward
        )
        high = lax.ppermute(lax.slice_in_dim(block, 0, width, axis=dim), axis, backward)
        block = jnp.concatenate([low, block, high], axis=dim)
    return block


def laplace(padded, depth_cells, width_cells):
    channel_count = padded.shape[0]
    inner_cells = padded[:, 1:-1, :]
    slab_rows = inner_cells.shape[1]
    block_view = inner_cells.reshape(channel_count, slab_rows, depth_cells, width_cells)
    extended = jnp.pad(block_view, ((0, 0), (0, 0), (1, 1), (1, 1)), mode="edge")
    beside_x = padded[:, 2:, :] + padded[:, :-2, :]
    beside_yz = (
        extended[:, :, 2:, 1:-1]
        + extended[:, :, :-2, 1:-1]
        + extended[:, :, 1:-1, 2:]
        + extended[:, :, 1:-1, :-2]
    )
    return beside_x + beside_yz.reshape(channel_count, slab_rows, -1) - 6.0 * inner_cells


def spread_biomass(biomass, motility):
    padded = extended_2(biomass, (("space", 1),), 1).astype(jnp.float32)
    return motility[:, None, None] * laplace(padded, NY, NZ)


def spread_resources(resources, diffusivity):
    padded = extended_2(resources, (("space", 1),), 1)
    return diffusivity[:, None, None] * laplace(padded, NY, NZ)


def per_device(
    biomass,
    resources,
    capacity,
    affinity,
    secretion,
    energy_yield,
    maintenance,
    motility,
    diffusivity,
    supply,
):
    local_strains, slab_rows, plane_cells = biomass.shape
    cells_dev = slab_rows * plane_cells
    seen = lax.all_gather(resources.astype(jnp.bfloat16), "species", axis=0, tiled=True)
    all_resources = seen.shape[0]
    seen_flat = seen.reshape(all_resources, cells_dev)
    mass_flat = biomass.reshape(local_strains, cells_dev)
    block_cells = math.gcd(256, cells_dev)
    block_count = cells_dev // block_cells

    def per_block(block_index, carry):
        growth_all, consumed_all, secreted_all = carry
        start = block_index * block_cells
        seen_block = lax.dynamic_slice_in_dim(seen_flat, start, block_cells, 1).astype(jnp.float32)
        mass_block = lax.dynamic_slice_in_dim(mass_flat, start, block_cells, 1).astype(jnp.float32)
        uptake = (
            capacity[:, :, None]
            * seen_block[None, :, :]
            / (affinity[:, :, None] + seen_block[None, :, :])
        )
        growth_block = jnp.sum(energy_yield[None, :, None] * uptake, axis=1) - maintenance[:, None]
        flux_block = jnp.sum(uptake, axis=1)
        product_block = (mass_block * flux_block).astype(jnp.bfloat16)
        consumed_block = jnp.sum(mass_block[:, None, :] * uptake, axis=0)
        secreted_block = jnp.dot(secretion, product_block, preferred_element_type=jnp.float32)
        growth_all = lax.dynamic_update_slice_in_dim(growth_all, growth_block, start, 1)
        consumed_all = lax.dynamic_update_slice_in_dim(consumed_all, consumed_block, start, 1)
        secreted_all = lax.dynamic_update_slice_in_dim(secreted_all, secreted_block, start, 1)
        return (growth_all, consumed_all, secreted_all)

    initial = (
        jnp.zeros((local_strains, cells_dev), jnp.float32),
        jnp.zeros((all_resources, cells_dev), jnp.float32),
        jnp.zeros((all_resources, cells_dev), jnp.float32),
    )
    growth_all, consumed_all, secreted_all = lax.fori_loop(0, block_count, per_block, initial)
    growth = growth_all.reshape(local_strains, slab_rows, plane_cells)
    consumed_all = consumed_all.reshape(all_resources, slab_rows, plane_cells)
    secreted_all = secreted_all.reshape(all_resources, slab_rows, plane_cells)
    consumed_owned, secreted_owned = (
        lax.psum_scatter(consumed_all, "species", scatter_dimension=0, tiled=True),
        lax.psum_scatter(secreted_all, "species", scatter_dimension=0, tiled=True),
    )
    net_owned = secreted_owned - consumed_owned
    mass_spread = spread_biomass(biomass, motility)
    resource_spread = spread_resources(resources, diffusivity)
    mass = biomass.astype(jnp.float32)
    new_biomass = mass + time_step * (mass * growth + mass_spread)
    new_resources = resources + time_step * (resource_spread + net_owned + supply[:, None, None])
    return (growth, new_biomass, new_resources)


def solution(mesh):
    return jax.shard_map(
        per_device,
        mesh=mesh,
        in_specs=(
            P("species", "space", None),
            P("species", "space", None),
            P("species", None),
            P("species", None),
            P(None, "species"),
            P(),
            P("species"),
            P("species"),
            P("species"),
            P("species"),
        ),
        out_specs=(
            P("species", "space", None),
            P("species", "space", None),
            P("species", "space", None),
        ),
        check_vma=False,
    )
```

profile of v0, /device:TPU:6, one launch (start us, length us, event | category | flops | bytes accessed | tf_op | source)
XLA Modules:
  0.0 374.1 jit_solution(9521856368249420357)
XLA Ops:
  7.2 0.0 all-reduce.5.cloned.1.call-start
  7.2 0.9 convert_element_type.30
  8.1 65.2 %all_gather.3 = bf16[128,2,1024]{2,1,0:T(2,128)(2,1)S(1)} all-gather(bf16[8,2,1024]{2,1,0:T(2,128)(2,1)S(1)} %convert_element_type.30), channel_id=1, replica_groups=mesh['space'=32,'species'=16] {'species'}, dimensions={0}, use_global_device_ids=true | all-gather | bytes 557056 | tf_op jit(solution)/shard_map/all_gather | solution.py:69
  73.4 0.1 copy.20
  73.5 0.0 copy-start.3
  73.6 0.0 copy-start.4
  73.6 0.0 copy-start.6
  73.6 0.0 copy-start.7
  73.6 0.1 broadcast.12
  73.7 0.1 broadcast.12.clone
  73.8 0.5 copy-done.3
  74.3 0.0 copy-done.4
  74.3 20.4 %while.17 = (s32[]{:T(128)}, f32[32,2048]{1,0:T(8,128)S(1)}, f32[128,2048]{1,0:T(8,128)S(1)}, f32[128,2048]{0,1:T(8,128)S(1)}, f32[128]{0:T(128)S(1)}, /*index=5...) while((s32[]{:T(128)}, f32[32,2048]{1,0:T(8,128)S(1)}, ...), condition=%wide.region_4.0_spmd, body=%wide.region_0.0_spmd.sunk | while | flops 10510342 | bytes 1157331 | solution.py:101
  74.4 2.2 fusion.32
  76.6 0.1 subtract_dynamic-update-slice_fusion.2
  76.6 0.2 fusion.33
  76.9 2.2 fusion.32
  79.1 0.1 subtract_dynamic-update-slice_fusion.2
  79.2 0.2 fusion.33
  79.5 2.2 fusion.32
  81.7 0.1 subtract_dynamic-update-slice_fusion.2
  81.8 0.2 fusion.33
  82.0 2.2 fusion.32
  84.2 0.1 subtract_dynamic-update-slice_fusion.2
  84.3 0.2 fusion.33
  84.6 2.2 fusion.32
  86.8 0.1 subtract_dynamic-update-slice_fusion.2
  86.9 0.2 fusion.33
  87.1 2.2 fusion.32
  89.3 0.1 subtract_dynamic-update-slice_fusion.2
  89.4 0.2 fusion.33
  89.7 2.2 fusion.32
  91.9 0.1 subtract_dynamic-update-slice_fusion.2
  92.0 0.2 fusion.33
  92.2 2.2 fusion.32
  94.4 0.1 subtract_dynamic-update-slice_fusion.2
  94.5 0.2 fusion.33
  94.7 1.9 reshape.50
  96.6 1.3 copy.19
  97.9 0.0 all-reduce.5.cloned.1.call-update
  97.9 0.2 fusion.25
  98.1 1.9 collective-permute-start.1
  100.0 2.4 collective-permute-start
  102.5 0.1 fusion.26
  102.5 3.2 collective-permute-start.3
  105.8 2.3 collective-permute-start.2
  108.1 0.1 reshape.47
  108.3 0.2 reshape.44
  108.5 0.0 copy-start.1
  108.6 0.1 fusion.23
  108.7 0.2 fusion.11
  108.9 0.1 reshape.48
  109.0 1.3 dynamic-slice
  111.0 0.4 maximum_convert_fusion
  111.4 0.1 slice.124
  111.5 0.3 reshape.45
  111.9 0.1 pad_maximum_fusion
  112.1 0.3 fusion.21
  112.3 0.7 fusion.3
  113.0 0.3 reshape.46
  113.3 0.0 copy-start.10
  113.3 1.2 convert_add_fusion
  114.5 251.0 %all-reduce.5.cloned.1.call-done = (f32[128,2,1024]{2,1,0:T(2,128)}, f32[128,2,1024]{2,1,0:T(2,128)}) async-done(((f32[128,2,1024]{2,1,0:T(2,128)}, f32[128,2,1024]{2,1,0:T(2,128)}), (f32[128,2,1024]{2,1,0:T(2,128)}, f32[128,2,1024]{2,1,0:T(2,128)})) %all-reduce.5.cloned.1.call-update) | async-done | bytes 2097168
  365.5 1.7 fusion.20
  (47 shorter events, 0.5 us)
Async XLA Ops:
  7.2 66.3 %copy-start = (bf16[32,2,1024]{2,1,0:T(2,128)(2,1)S(1)}, bf16[32,2,1024]{2,1,0:T(2,128)(2,1)}, u32[]{:S(2)}) copy-start(bf16[32,2,1024]{2,1,0:T(2,128)(2,1)} %param.12) | copy-start | bytes 393220
  7.2 358.4 %all-reduce.5.cloned.1.call-start = ((), (), s32[]{:S(2)}) async-start(), calls=%async_computation | async-start | bytes 4194304
  73.5 0.7 copy-start.3
  73.6 0.7 copy-start.4
  73.6 0.7 copy-start.5
  73.6 0.7 copy-start.6
  73.6 0.7 copy-start.7
  97.9 4.6 %copy-start.2 = (f32[8,2,1024]{2,1,0:T(2,128)S(1)}, f32[8,2,1024]{2,1,0:T(2,128)}, u32[]{:S(2)}) copy-start(f32[8,2,1024]{2,1,0:T(2,128)} %param.13) | copy-start | bytes 196612
  98.1 12.8 %collective-permute-start.1 = (bf16[32,1,1024]{2,1,0:T(2,128)(2,1)S(1)}, bf16[32,1,1024]{2,1,0:T(2,128)(2,1)S(1)}, u32[]{:S(2)}, u32[]{:S(2)}) collective-permute-start(bf16[32,1,1024]{2,1,0:T(2,128)(2,1)S(1)} %get-tuple-element.261), channel_id=1, source_target_pairs={{16,0},{32,16},{48,32},{64,48},{80,64},{96,80},{112,96},{128,112},... | collective-permute-start | bytes 196616 | tf_op jit(solution)/shard_map/ppermute | solution.py:24
  100.0 10.9 %collective-permute-start = (bf16[32,1,1024]{2,1,0:T(2,128)(2,1)S(1)}, bf16[32,1,1024]{2,1,0:T(2,128)(2,1)S(1)}, u32[]{:S(2)}, u32[]{:S(2)}) collective-permute-start(bf16[32,1,1024]{2,1,0:T(2,128)(2,1)S(1)} %get-tuple-element.260), channel_id=1, source_target_pairs={{0,16},{16,32},{32,48},{48,64},{64,80},{80,96},{96,112},{112,128},... | collective-permute-start | bytes 196616 | tf_op jit(solution)/shard_map/ppermute | solution.py:21
  102.5 12.0 %collective-permute-start.3 = (f32[8,1,1024]{2,1,0:T(1,128)S(1)}, f32[8,1,1024]{2,1,0:T(1,128)S(1)}, u32[]{:S(2)}, u32[]{:S(2)}) collective-permute-start(f32[8,1,1024]{2,1,0:T(1,128)S(1)} %get-tuple-element.263), channel_id=1, source_target_pairs={{0,16},{16,32},{32,48},{48,64},{64,80},{80,96},{96,112},{112,128},... | collective-permute-start | bytes 98312 | tf_op jit(solution)/shard_map/ppermute | solution.py:21
  105.8 8.8 %collective-permute-start.2 = (f32[8,1,1024]{2,1,0:T(1,128)S(1)}, f32[8,1,1024]{2,1,0:T(1,128)S(1)}, u32[]{:S(2)}, u32[]{:S(2)}) collective-permute-start(f32[8,1,1024]{2,1,0:T(1,128)S(1)} %get-tuple-element.262), channel_id=1, source_target_pairs={{16,0},{32,16},{48,32},{64,48},{80,64},{96,80},{112,96},{128,112},... | collective-permute-start | bytes 98312 | tf_op jit(solution)/shard_map/ppermute | solution.py:24
  108.5 4.8 %copy-start.1 = (f32[32,2,1024]{2,1,0:T(2,128)}, f32[32,2,1024]{2,1,0:T(2,128)S(1)}, u32[]{:S(2)}) copy-start(f32[32,2,1024]{2,1,0:T(2,128)S(1)} %reshape.44) | copy-start | bytes 786436
  112.3 0.9 copy-start.8
  113.3 252.3 %copy-start.9 = (f32[8]{0:T(128)S(1)}, f32[8]{0:T(128)}, u32[]{:S(2)}) copy-start(f32[8]{0:T(128)} %param.21) | copy-start | bytes 100
  113.3 252.3 %copy-start.10 = (f32[8]{0:T(128)S(1)}, f32[8]{0:T(128)}, u32[]{:S(2)}) copy-start(f32[8]{0:T(128)} %param.20) | copy-start | bytes 100
Sparse Core Ops, SparseCore 0:
  98.0 267.4 all-reduce.4
where the time goes:
time: 376 us; the launch traced here: 374 us
  waiting for transfers between devices  251 us (67%)
  blocking collectives  65.2 us (17%)
  other arithmetic  23.6 us (6%)
  between operations  15 us (4%)
  starting transfers between devices  9.93 us (3%)
  local copies, waits for them, and re-layouts  7.3 us (2%)
    unnamed x2, waiting for transfers between devices  251 us
    all_gather x1, blocking collectives, per_device(): lax.all_gather(resources.astype(jnp.bfloat16), 'species', axis=0, tiled=T...  65.2 us
    reduce_sum x8, other arithmetic, per_block(): flux_block = jnp.sum(uptake, axis=1)  17.5 us
  transfers between devices with their start and end apart: 5, of which 1 were waited for; matrix products, arithmetic and copies ran while one was open for 2% of the time, Pallas kernels for 0%

commit v1 on v0

v1 whole, which is shorter than its diff:
```python
import functools

import jax
import jax.numpy as jnp
from jax import lax
from jax.experimental import pallas as pl
from jax.experimental.pallas import tpu as pltpu
from jax.sharding import PartitionSpec as P

MESH = pl.DeviceIdType.MESH
RING = 4
PARTS = 4
TIME_STEP = 0.25
ROWS = 16
LANES = 128


def laplace(field, low, high):
    row = lax.broadcasted_iota(jnp.int32, (ROWS, LANES), 0)
    lane = lax.broadcasted_iota(jnp.int32, (ROWS, LANES), 1)
    odd = lax.rem(row, 2) == 1
    z = lax.rem(lane, 64)
    both = field + jnp.where(odd, low, high)
    beside_x = jnp.where(odd, pltpu.roll(both, 1, 0), pltpu.roll(both, ROWS - 1, 0))
    up = jnp.where(z == 63, field, pltpu.roll(field, LANES - 1, 1))
    down = jnp.where(z == 0, field, pltpu.roll(field, 1, 1))
    half = pltpu.roll(field, 64, 1)
    before = jnp.where(row < 2, field, pltpu.roll(half, 2, 0))
    after = jnp.where(row >= ROWS - 2, field, pltpu.roll(half, ROWS - 2, 0))
    beside_y = half + jnp.where(lane < 64, before, after)
    return beside_x + (beside_y + (up + down)) - 6.0 * field


def kernel(
    n_space,
    biomass,
    resources,
    capacity,
    affinity,
    secretion,
    energy_yield,
    maintenance,
    motility,
    diffusivity,
    supply,
    growth_out,
    biomass_out,
    resources_out,
    seen,
    mass,
    cap_rows,
    aff_rows,
    flux,
    gain,
    consumed,
    product,
    net,
    relay_y,
    sum_y,
    reduced,
    relay_z,
    sum_z,
    final,
    halo_b,
    halo_r,
    send_sem,
    recv_sem,
):
    strains = biomass.shape[0]
    block = resources.shape[0]
    blocks = RING * RING
    half = block // 2
    me = lax.axis_index("species")
    place = lax.axis_index("space")
    y, h = lax.div(me, RING), lax.rem(me, RING)
    y_up, y_dn, y_op = (lax.rem(y + k, RING) for k in (1, 3, 2))
    h_up, h_dn, h_op = (lax.rem(h + k, RING) for k in (1, 3, 2))
    to_y_up = {"species": y_up * RING + h}
    to_y_dn = {"species": y_dn * RING + h}
    to_h_up = {"species": y * RING + h_up}
    to_h_dn = {"species": y * RING + h_dn}
    to_next = {"space": lax.rem(place + 1, n_space)}
    to_prev = {"space": lax.rem(place + n_space - 1, n_space)}

    barrier = pltpu.get_barrier_semaphore()
    for target in (to_h_up, to_h_dn, to_y_up, to_y_dn, to_next, to_prev):
        pl.semaphore_signal(barrier, inc=1, device_id=target, device_id_type=MESH)

    seen[me] = resources[...].astype(jnp.bfloat16)
    mass[...] = biomass[...].astype(jnp.float32)
    pad = jnp.zeros((LANES - strains, LANES), jnp.float32)
    cap_t = jnp.concatenate([capacity[...], pad], axis=0).T
    aff_t = jnp.concatenate([affinity[...], pad], axis=0).T
    for s in range(strains):
        cap_rows[s] = jnp.broadcast_to(cap_t[:, s : s + 1], (LANES, LANES))
        aff_rows[s] = jnp.broadcast_to(aff_t[:, s : s + 1], (LANES, LANES))
    sec_pad = jnp.zeros((LANES - strains, LANES), jnp.float32)
    sec = jnp.concatenate([secretion[...].astype(jnp.float32), sec_pad], axis=0).T
    sec = sec[:, :strains].astype(jnp.bfloat16)
    flux[...] = jnp.zeros_like(flux)
    gain[...] = jnp.zeros_like(gain)

    pl.semaphore_wait(barrier, 6)

    started = []

    def copy(index, src, dst, target):
        return pltpu.make_async_remote_copy(
            src_ref=src,
            dst_ref=dst,
            send_sem=send_sem.at[index],
            recv_sem=recv_sem.at[index],
            device_id=target,
            device_id_type=MESH,
        )

    def start(index, src, dst, target):
        c = copy(index, src, dst, target)
        c.start()
        started.append(c)

    def arrived(index, ref):
        copy(index, ref, ref, to_y_up).wait_recv()

    def whole(b):
        return seen.at[b]

    def low_half(b):
        return seen.at[b, pl.ds(0, half)]

    def high_half(b):
        return seen.at[b, pl.ds(half, half)]

    def at(yy, hh):
        return yy * RING + hh

    def y_send(column, hh):
        start(4 + 4 * column, whole(at(y, hh)), whole(at(y, hh)), to_y_up)
        start(5 + 4 * column, whole(at(y, hh)), whole(at(y, hh)), to_y_dn)

    def y_pass(column, hh):
        arrived(4 + 4 * column, whole(at(y_dn, hh)))
        part = low_half(at(y_dn, hh))
        start(6 + 4 * column, part, part, to_y_up)
        arrived(5 + 4 * column, whole(at(y_up, hh)))
        part = high_half(at(y_up, hh))
        start(7 + 4 * column, part, part, to_y_dn)

    def y_last(column, hh):
        arrived(6 + 4 * column, low_half(at(y_op, hh)))
        arrived(7 + 4 * column, high_half(at(y_op, hh)))

    def compute(b):
        xs = [seen[b, r].astype(jnp.float32) for r in range(block)]
        es = [energy_yield[b * block + r] for r in range(block)]

        def strain(s, sums):
            m = mass[s]
            f = flux[s]
            g = gain[s]
            out = []
            for r in range(block):
                row = pl.ds(b * block + r, 1)
                a = jnp.broadcast_to(aff_rows[s, row, :], (ROWS, LANES))
                c = jnp.broadcast_to(cap_rows[s, row, :], (ROWS, LANES))
                v = c / (a + xs[r])
                out.append(sums[r] + m * v)
                u = xs[r] * v
                f = f + u
                g = g + es[r] * u
            flux[s] = f
            gain[s] = g
            return tuple(out)

        zero = jnp.zeros((ROWS, LANES), jnp.float32)
        sums = lax.fori_loop(0, strains, strain, (zero,) * block)
        for r in range(block):
            consumed[pl.ds((b * block + r) * ROWS, ROWS), :] = sums[r] * xs[r]

    start(0, whole(me), whole(me), to_h_up)
    start(1, whole(me), whole(me), to_h_dn)
    y_send(0, h)
    compute(me)
    y_pass(0, h)
    compute(at(y_dn, h))
    compute(at(y_up, h))
    y_last(0, h)
    compute(at(y_op, h))
    arrived(0, whole(at(y, h_dn)))
    start(2, low_half(at(y, h_dn)), low_half(at(y, h_dn)), to_h_up)
    y_send(1, h_dn)
    arrived(1, whole(at(y, h_up)))
    start(3, high_half(at(y, h_up)), high_half(at(y, h_up)), to_h_dn)
    y_send(2, h_up)
    compute(at(y, h_dn))
    compute(at(y, h_up))
    y_pass(1, h_dn)
    y_pass(2, h_up)
    compute(at(y_dn, h_dn))
    compute(at(y_up, h_dn))
    compute(at(y_dn, h_up))
    compute(at(y_up, h_up))
    arrived(2, low_half(at(y, h_op)))
    part = low_half(at(y, h_op))
    start(16, part, part, to_y_up)
    start(17, part, part, to_y_dn)
    arrived(3, high_half(at(y, h_op)))
    part = high_half(at(y, h_op))
    start(18, part, part, to_y_up)
    start(19, part, part, to_y_dn)
    y_last(1, h_dn)
    y_last(2, h_up)
    compute(at(y_op, h_dn))
    compute(at(y_op, h_up))
    compute(at(y, h_op))
    arrived(16, low_half(at(y_dn, h_op)))
    start(20, low_half(at(y_dn, h_op)), low_half(at(y_dn, h_op)), to_y_up)
    arrived(19, high_half(at(y_up, h_op)))
    start(21, high_half(at(y_up, h_op)), high_half(at(y_up, h_op)), to_y_dn)
    start(22, biomass, halo_b.at[0], to_next)
    start(23, biomass, halo_b.at[1], to_prev)
    start(24, resources, halo_r.at[0], to_next)
    start(25, resources, halo_r.at[1], to_prev)
    arrived(18, high_half(at(y_dn, h_op)))
    compute(at(y_dn, h_op))
    arrived(17, low_half(at(y_up, h_op)))
    compute(at(y_up, h_op))
    arrived(20, low_half(at(y_op, h_op)))
    arrived(21, high_half(at(y_op, h_op)))
    compute(at(y_op, h_op))

    def to_product(s, _):
        value = (mass[s] * flux[s]).astype(jnp.bfloat16).astype(jnp.float32)
        product[pl.ds(s * ROWS, ROWS), :] = value
        return 0

    lax.fori_loop(0, strains, to_product, 0)

    rows = ROWS // PARTS
    first = rows // 2
    base = 26

    def lo(p):
        return pl.ds(p * rows, first)

    def hi(p):
        return pl.ds(p * rows + first, rows - first)

    def al(p):
        return pl.ds(p * rows, rows)

    def run(yy):
        return pl.ds(yy * RING, RING)

    for p in range(PARTS):
        for q in range(p * rows, (p + 1) * rows):
            made = product[pl.ds(q, strains, stride=ROWS), :].astype(jnp.bfloat16)
            secreted = jnp.dot(sec, made, preferred_element_type=jnp.float32)
            used = consumed[pl.ds(q, blocks * block, stride=ROWS), :]
            net[q] = (secreted - used).reshape(blocks, block, LANES)
        k = base + 8 * p
        start(k, net.at[lo(p), run(y_op)], relay_y.at[lo(p)], to_y_up)
        start(k + 1, net.at[hi(p), run(y_op)], relay_y.at[hi(p)], to_y_dn)

    for p in range(PARTS):
        k = base + 8 * p
        arrived(k, relay_y.at[lo(p)])
        net[lo(p), run(y_up)] = net[lo(p), run(y_up)] + relay_y[lo(p)]
        start(k + 2, net.at[al(p), run(y_up)], sum_y.at[0, al(p)], to_y_up)
        arrived(k + 1, relay_y.at[hi(p)])
        net[hi(p), run(y_dn)] = net[hi(p), run(y_dn)] + relay_y[hi(p)]
        start(k + 3, net.at[al(p), run(y_dn)], sum_y.at[1, al(p)], to_y_dn)

    arrived(22, halo_b.at[0])
    arrived(23, halo_b.at[1])

    def update(s, _):
        m = mass[s]
        grown = gain[s] - maintenance[s]
        low = halo_b[0, s].astype(jnp.float32)
        high = halo_b[1, s].astype(jnp.float32)
        growth_out[s] = grown
        spread = motility[s] * laplace(m, low, high)
        biomass_out[s] = m + TIME_STEP * (m * grown + spread)
        return 0

    lax.fori_loop(0, strains, update, 0)

    for p in range(PARTS):
        k = base + 8 * p
        arrived(k + 2, sum_y.at[0, al(p)])
        arrived(k + 3, sum_y.at[1, al(p)])
        reduced[al(p)] = net[al(p), run(y)] + (sum_y[0, al(p)] + sum_y[1, al(p)])
        start(k + 4, reduced.at[lo(p), h_op], relay_z.at[lo(p)], to_h_up)
        start(k + 5, reduced.at[hi(p), h_op], relay_z.at[hi(p)], to_h_dn)

    for p in range(PARTS):
        k = base + 8 * p
        arrived(k + 4, relay_z.at[lo(p)])
        reduced[lo(p), h_up] = reduced[lo(p), h_up] + relay_z[lo(p)]
        start(k + 6, reduced.at[al(p), h_up], sum_z.at[0, al(p)], to_h_up)
        arrived(k + 5, relay_z.at[hi(p)])
        reduced[hi(p), h_dn] = reduced[hi(p), h_dn] + relay_z[hi(p)]
        start(k + 7, reduced.at[al(p), h_dn], sum_z.at[1, al(p)], to_h_dn)

    arrived(24, halo_r.at[0])
    arrived(25, halo_r.at[1])
    for p in range(PARTS):
        k = base + 8 * p
        arrived(k + 6, sum_z.at[0, al(p)])
        arrived(k + 7, sum_z.at[1, al(p)])
        for q in range(p * rows, (p + 1) * rows):
            total = reduced[q, h] + (sum_z[0, q] + sum_z[1, q])
            final[pl.ds(q, block, stride=ROWS), :] = total
    for r in range(block):
        value = resources[r]
        spread = diffusivity[r] * laplace(value, halo_r[0, r], halo_r[1, r])
        released = final[pl.ds(r * ROWS, ROWS), :]
        resources_out[r] = value + TIME_STEP * (spread + released + supply[r])

    for c in started:
        c.wait_send()


def per_device(
    biomass,
    resources,
    capacity,
    affinity,
    secretion,
    energy_yield,
    maintenance,
    motility,
    diffusivity,
    supply,
    n_space,
):
    strains, slab, plane = biomass.shape
    block = resources.shape[0]
    blocks = RING * RING
    tiles = plane // LANES

    def split(field):
        parts = field.reshape(field.shape[0], slab, tiles, LANES)
        return parts.transpose(0, 2, 1, 3).reshape(field.shape[0], ROWS, LANES)

    def join(field):
        parts = field.reshape(field.shape[0], tiles, slab, LANES)
        return parts.transpose(0, 2, 1, 3).reshape(field.shape[0], slab, plane)

    f32 = jnp.float32
    vmem = pl.BlockSpec(memory_space=pltpu.VMEM)
    smem = pl.BlockSpec(memory_space=pltpu.SMEM)
    copies = 26 + 8 * PARTS
    outs = pl.pallas_call(
        functools.partial(kernel, n_space),
        out_shape=(
            jax.ShapeDtypeStruct((strains, ROWS, LANES), f32),
            jax.ShapeDtypeStruct((strains, ROWS, LANES), f32),
            jax.ShapeDtypeStruct((block, ROWS, LANES), f32),
        ),
        in_specs=[vmem] * 5 + [smem] * 5,
        out_specs=(vmem,) * 3,
        scratch_shapes=[
            pltpu.VMEM((blocks, block, ROWS, LANES), jnp.bfloat16),
            pltpu.VMEM((strains, ROWS, LANES), f32),
            pltpu.VMEM((strains, LANES, LANES), f32),
            pltpu.VMEM((strains, LANES, LANES), f32),
            pltpu.VMEM((strains, ROWS, LANES), f32),
            pltpu.VMEM((strains, ROWS, LANES), f32),
            pltpu.VMEM((blocks * block * ROWS, LANES), f32),
            pltpu.VMEM((strains * ROWS, LANES), f32),
            pltpu.VMEM((ROWS, blocks, block, LANES), f32),
            pltpu.VMEM((ROWS, RING, block, LANES), f32),
            pltpu.VMEM((2, ROWS, RING, block, LANES), f32),
            pltpu.VMEM((ROWS, RING, block, LANES), f32),
            pltpu.VMEM((ROWS, block, LANES), f32),
            pltpu.VMEM((2, ROWS, block, LANES), f32),
            pltpu.VMEM((block * ROWS, LANES), f32),
            pltpu.VMEM((2, strains, ROWS, LANES), jnp.bfloat16),
            pltpu.VMEM((2, block, ROWS, LANES), f32),
            pltpu.SemaphoreType.DMA((copies,)),
            pltpu.SemaphoreType.DMA((copies,)),
        ],
        compiler_params=pltpu.CompilerParams(
            collective_id=0, has_side_effects=True, vmem_limit_bytes=32 << 20
        ),
    )(
        split(biomass),
        split(resources),
        capacity,
        affinity,
        secretion.T,
        energy_yield,
        maintenance,
        motility,
        diffusivity,
        supply,
    )
    return tuple(join(out) for out in outs)


def solution(mesh):
    return jax.shard_map(
        functools.partial(per_device, n_space=mesh.shape["space"]),
        mesh=mesh,
        in_specs=(
            P("species", "space", None),
            P("species", "space", None),
            P("species", None),
            P("species", None),
            P(None, "species"),
            P(),
            P("species"),
            P("species"),
            P("species"),
            P("species"),
        ),
        out_specs=(
            P("species", "space", None),
            P("species", "space", None),
            P("species", "space", None),
        ),
        check_vma=False,
    )
```

time: 376 us -> 67.6 us (0.18)
  waiting for transfers between devices: 251 us -> 0 us
  blocking collectives: 65.2 us -> 0 us
  Pallas kernels: 0 us -> 59.9 us
  other arithmetic: 23.6 us -> 0 us
  between operations: 15 us -> 0.69 us
  starting transfers between devices: 9.93 us -> 0 us
    unnamed x2 -> x0, waiting for transfers between devices: 251 us -> none
    all_gather x1 -> x0, blocking collectives: 65.2 us -> none  [per_device(): lax.all_gather(resources.astype(jnp.bfloat16), 'species', axis=0, tiled=T...]
    pallas_call x0 -> x1, Pallas kernels: none -> 59.9 us  [per_device(): pl.pallas_call(functools.partial(kernel, n_space), out_shape=(jax.ShapeDt...]
    reduce_sum x8 -> x0, other arithmetic: 17.5 us -> none  [per_block(): flux_block = jnp.sum(uptake, axis=1)]
    ppermute x4 -> x0, starting transfers between devices: 9.89 us -> none  [the longest x2 5.63 us: extended_2(): lax.ppermute(lax.slice_in_dim(block, block.shape[dim] - width, None, axis...]
    unnamed x25 -> x23, local copies, waits for them, and re-layouts: 1.97 us -> 6.59 us
    reshape x7 -> x0, local copies, waits for them, and re-layouts: 4.23 us -> none  [the longest x1 1.86 us: per_device(): consumed_all = consumed_all.reshape(all_resources, slab_rows, plane_cells)]
    add x4 -> x0, other arithmetic: 3.77 us -> none  [the longest x1 1.7 us: per_device(): resources + time_step * (resource_spread + net_owned + supply[:, None, No...]
  transfers between devices with their start and end apart: 5 -> 0, of which waited for: 1 -> 0; matrix products, arithmetic and copies ran while one was open for 2% -> 0% of each run, Pallas kernels for 0% -> 0%
where the time goes in v1:
time: 67.6 us; the launch traced here: 67.2 us
  Pallas kernels  59.9 us (89%)
  local copies, waits for them, and re-layouts  6.59 us (10%)
  between operations  0.69 us (1%)
    pallas_call x1, Pallas kernels, per_device(): pl.pallas_call(functools.partial(kernel, n_space), out_shape=(jax.ShapeDt...  59.9 us
    unnamed x23, local copies, waits for them, and re-layouts  6.59 us

profile of v1, /device:TPU:6, one launch (start us, length us, event | category | flops | bytes accessed | tf_op | source)
XLA Modules:
  0.0 67.2 jit_solution(13703518675367409796)
XLA Ops:
  0.6 0.0 copy-start.8
  0.6 0.0 copy-start.9
  0.7 0.0 copy-start.5
  0.7 0.0 copy-start.6
  0.7 0.0 copy-start.7
  0.7 0.6 copy-done.8
  1.3 0.0 copy-done.9
  1.3 0.0 copy-done.5
  1.3 0.0 copy-done.6
  1.3 0.0 copy-done.7
  1.4 0.0 copy-start
  1.4 0.9 %copy-done = bf16[32,2,1024]{2,1,0:T(2,128)(2,1)S(1)} copy-done((bf16[32,2,1024]{2,1,0:T(2,128)(2,1)S(1)}, bf16[32,2,1024]{2,1,0:T(2,128)(2,1)}, u32[]{:S(2)}) %copy-start) | copy-done | bytes 131096
  2.3 0.0 copy-start.1
  2.3 0.8 %copy-done.1 = f32[8,2,1024]{2,1,0:T(2,128)S(1)} copy-done((f32[8,2,1024]{2,1,0:T(2,128)S(1)}, f32[8,2,1024]{2,1,0:T(2,128)}, u32[]{:S(2)}) %copy-start.1) | copy-done | bytes 65560
  3.1 0.0 copy-start.2
  3.1 0.7 %copy-done.2 = f32[32,128]{1,0:T(8,128)S(1)} copy-done((f32[32,128]{1,0:T(8,128)S(1)}, f32[32,128]{1,0:T(8,128)}, u32[]{:S(2)}) %copy-start.2) | copy-done | bytes 16408
  3.8 0.0 copy-start.3
  3.8 0.7 %copy-done.3 = f32[32,128]{1,0:T(8,128)S(1)} copy-done((f32[32,128]{1,0:T(8,128)S(1)}, f32[32,128]{1,0:T(8,128)}, u32[]{:S(2)}) %copy-start.3) | copy-done | bytes 16408
  4.5 0.0 copy-start.4
  4.5 0.7 %copy-done.4 = bf16[128,32]{0,1:T(8,128)(2,1)S(1)} copy-done((bf16[128,32]{0,1:T(8,128)(2,1)S(1)}, bf16[128,32]{0,1:T(8,128)(2,1)}, u32[]{:S(2)}) %copy-start.4) | copy-done | bytes 8216
  5.2 59.9 %shard_map.121 = (f32[32,16,128]{2,1,0:T(8,128)S(1)}, f32[32,16,128]{2,1,0:T(8,128)S(1)}, f32[8,16,128]{2,1,0:T(8,128)S(1)}) custom-call(bf16[32,16,128]{2,1,0:T(8,128)(2,1)S(1)} %bitcast.28, f32[8,16,128]{2,1,0:T(8,128)S(1)} %bitcast.30, f32[32,128]{1,0:T(8,128)S(1)} %copy-done.2, f32[32,128]{1,0:T(8,128)S(1)} %copy-done.3, bf16[32,128]{1,0:T(8,128)(2,1)S(1)} %bitcast.31, ...), custom_call_target="tpu_custom_call" | custom-call | tf_op jit(solution)/shard_map/pallas_call | solution.py:355
  65.2 0.7 %copy.21 = f32[32,2,1024]{2,1,0:T(2,128)} copy(f32[32,2,1024]{2,1,0:T(2,128)S(1)} %bitcast.27) | data formatting | bytes 524288
  65.9 0.7 %copy.22 = f32[32,2,1024]{2,1,0:T(2,128)} copy(f32[32,2,1024]{2,1,0:T(2,128)S(1)} %bitcast.26) | data formatting | bytes 524288
  66.6 0.6 copy.23
Async XLA Ops:
  0.6 0.7 copy-start.8
  0.6 0.7 copy-start.9
  0.7 0.7 copy-start.5
  0.7 0.7 %copy-start.6 = (f32[32]{0:T(128)S(1)}, f32[32]{0:T(128)}, u32[]{:S(2)}) copy-start(f32[32]{0:T(128)} %maintenance.1) | copy-start | bytes 388
  0.7 0.7 %copy-start.7 = (f32[32]{0:T(128)S(1)}, f32[32]{0:T(128)}, u32[]{:S(2)}) copy-start(f32[32]{0:T(128)} %motility.1) | copy-start | bytes 388
  1.4 0.9 %copy-start = (bf16[32,2,1024]{2,1,0:T(2,128)(2,1)S(1)}, bf16[32,2,1024]{2,1,0:T(2,128)(2,1)}, u32[]{:S(2)}) copy-start(bf16[32,2,1024]{2,1,0:T(2,128)(2,1)} %param.10) | copy-start | bytes 393220
  2.3 0.8 %copy-start.1 = (f32[8,2,1024]{2,1,0:T(2,128)S(1)}, f32[8,2,1024]{2,1,0:T(2,128)}, u32[]{:S(2)}) copy-start(f32[8,2,1024]{2,1,0:T(2,128)} %param.11) | copy-start | bytes 196612
  3.1 0.7 %copy-start.2 = (f32[32,128]{1,0:T(8,128)S(1)}, f32[32,128]{1,0:T(8,128)}, u32[]{:S(2)}) copy-start(f32[32,128]{1,0:T(8,128)} %capacity.1) | copy-start | bytes 49156
  3.8 0.7 %copy-start.3 = (f32[32,128]{1,0:T(8,128)S(1)}, f32[32,128]{1,0:T(8,128)}, u32[]{:S(2)}) copy-start(f32[32,128]{1,0:T(8,128)} %affinity.1) | copy-start | bytes 49156
  4.5 0.7 %copy-start.4 = (bf16[128,32]{0,1:T(8,128)(2,1)S(1)}, bf16[128,32]{0,1:T(8,128)(2,1)}, u32[]{:S(2)}) copy-start(bf16[128,32]{0,1:T(8,128)(2,1)} %param.14) | copy-start | bytes 24580

commit v2 on v1

v2 whole, which is shorter than its diff:
```python
import functools

import jax
import jax.numpy as jnp
from jax import lax
from jax.experimental import pallas as pl
from jax.experimental.pallas import tpu as pltpu
from jax.sharding import PartitionSpec as P

MESH = pl.DeviceIdType.MESH
RING = 4
GROUP = 4
UNROLL = 8
PARTS = 4
TIME_STEP = 0.25
SMALL = 2.0**-6
STEPS = 19.5
BOTTOM = 125.0
ROWS = 16
LANES = 128


def laplace(field, low, high):
    row = lax.broadcasted_iota(jnp.int32, (ROWS, LANES), 0)
    lane = lax.broadcasted_iota(jnp.int32, (ROWS, LANES), 1)
    odd = lax.rem(row, 2) == 1
    z = lax.rem(lane, 64)
    both = field + jnp.where(odd, low, high)
    beside_x = jnp.where(odd, pltpu.roll(both, 1, 0), pltpu.roll(both, ROWS - 1, 0))
    up = jnp.where(z == 63, field, pltpu.roll(field, LANES - 1, 1))
    down = jnp.where(z == 0, field, pltpu.roll(field, 1, 1))
    half = pltpu.roll(field, 64, 1)
    before = jnp.where(row < 2, field, pltpu.roll(half, 2, 0))
    after = jnp.where(row >= ROWS - 2, field, pltpu.roll(half, ROWS - 2, 0))
    beside_y = half + jnp.where(lane < 64, before, after)
    return beside_x + (beside_y + (up + down)) - 6.0 * field


def encode(value):
    level = jnp.log2(jnp.abs(value) * (1.0 / SMALL) + 1.0)
    code = jnp.exp2(level * STEPS - BOTTOM)
    return jnp.where(value < 0.0, -code, code).astype(jnp.bfloat16)


def decode(code):
    code = code.astype(jnp.float32)
    level = (jnp.log2(jnp.abs(code)) + BOTTOM) * (1.0 / STEPS)
    value = jnp.exp2(level) * SMALL - SMALL
    return jnp.where(code < 0.0, -value, value)


def kernel(
    n_space,
    biomass_in,
    resources_in,
    capacity_in,
    affinity_in,
    secretion_in,
    energy_yield_in,
    maintenance_in,
    motility_in,
    diffusivity_in,
    supply_in,
    growth_hbm,
    biomass_hbm,
    resources_hbm,
    biomass,
    resources,
    capacity,
    affinity,
    secretion,
    energy_yield,
    maintenance,
    motility,
    diffusivity,
    supply,
    seen,
    mass,
    cap_rows,
    aff_rows,
    flux,
    gain,
    consumed,
    product,
    net,
    pass_y,
    relay_y,
    send_y,
    sum_y,
    reduced,
    pass_z,
    relay_z,
    send_z,
    sum_z,
    final,
    halo_b,
    halo_r,
    send_sem,
    recv_sem,
    load_sem,
    store_sem,
    growth_out,
    biomass_out,
    resources_out,
):
    strains = biomass.shape[0]
    block = resources.shape[0]
    blocks = RING * RING
    half = block // 2
    me = lax.axis_index("species")
    place = lax.axis_index("space")
    y, h = lax.div(me, RING), lax.rem(me, RING)
    y_up, y_dn, y_op = (lax.rem(y + k, RING) for k in (1, 3, 2))
    h_up, h_dn, h_op = (lax.rem(h + k, RING) for k in (1, 3, 2))
    to_y_up = {"species": y_up * RING + h}
    to_y_dn = {"species": y_dn * RING + h}
    to_h_up = {"species": y * RING + h_up}
    to_h_dn = {"species": y * RING + h_dn}
    to_next = {"space": lax.rem(place + 1, n_space)}
    to_prev = {"space": lax.rem(place + n_space - 1, n_space)}

    barrier = pltpu.get_barrier_semaphore()
    for target in (to_h_up, to_h_dn, to_y_up, to_y_dn, to_next, to_prev):
        pl.semaphore_signal(barrier, inc=1, device_id=target, device_id_type=MESH)

    pairs = (
        (resources_in, resources),
        (biomass_in, biomass),
        (capacity_in, capacity),
        (affinity_in, affinity),
        (secretion_in, secretion),
        (energy_yield_in, energy_yield),
        (maintenance_in, maintenance),
        (motility_in, motility),
        (diffusivity_in, diffusivity),
        (supply_in, supply),
    )
    loads = [
        pltpu.make_async_copy(src, dst, load_sem.at[i])
        for i, (src, dst) in enumerate(pairs)
    ]
    for load in loads:
        load.start()
    loads[0].wait()
    seen[me] = resources[...].astype(jnp.bfloat16)

    pl.semaphore_wait(barrier, 6)

    started = []

    def copy(index, src, dst, target):
        return pltpu.make_async_remote_copy(
            src_ref=src,
            dst_ref=dst,
            send_sem=send_sem.at[index],
            recv_sem=recv_sem.at[index],
            device_id=target,
            device_id_type=MESH,
        )

    def start(index, src, dst, target):
        c = copy(index, src, dst, target)
        c.start()
        started.append(c)

    def arrived(index, ref):
        copy(index, ref, ref, to_y_up).wait_recv()

    def whole(b):
        return seen.at[b]

    def low_half(b):
        return seen.at[b, pl.ds(0, half)]

    def high_half(b):
        return seen.at[b, pl.ds(half, half)]

    def at(yy, hh):
        return yy * RING + hh

    def y_send(column, hh):
        start(4 + 4 * column, whole(at(y, hh)), whole(at(y, hh)), to_y_up)
        start(5 + 4 * column, whole(at(y, hh)), whole(at(y, hh)), to_y_dn)

    def y_pass(column, hh):
        arrived(4 + 4 * column, whole(at(y_dn, hh)))
        part = low_half(at(y_dn, hh))
        start(6 + 4 * column, part, part, to_y_up)
        arrived(5 + 4 * column, whole(at(y_up, hh)))
        part = high_half(at(y_up, hh))
        start(7 + 4 * column, part, part, to_y_dn)

    def y_last(column, hh):
        arrived(6 + 4 * column, low_half(at(y_op, hh)))
        arrived(7 + 4 * column, high_half(at(y_op, hh)))

    def compute(b):
        def quarter(part, _):
            first_r = part * GROUP
            xs = [seen[b, first_r + r].astype(jnp.float32) for r in range(GROUP)]
            es = [energy_yield[b * block + first_r + r] for r in range(GROUP)]

            def strain(i, sums):
                sums = list(sums)
                for k in range(UNROLL):
                    s = i * UNROLL + k
                    m = mass[s]
                    f = flux[s]
                    g = gain[s]
                    for r in range(GROUP):
                        row = pl.ds(b * block + first_r + r, 1)
                        a = jnp.broadcast_to(aff_rows[s, row, :], (ROWS, LANES))
                        c = jnp.broadcast_to(cap_rows[s, row, :], (ROWS, LANES))
                        v = c / (a + xs[r])
                        sums[r] = sums[r] + m * v
                        u = xs[r] * v
                        f = f + u
                        g = g + es[r] * u
                    flux[s] = f
                    gain[s] = g
                return tuple(sums)

            zero = jnp.zeros((ROWS, LANES), jnp.float32)
            sums = lax.fori_loop(0, strains // UNROLL, strain, (zero,) * GROUP)
            for r in range(GROUP):
                row = pl.multiple_of((b * block + first_r + r) * ROWS, ROWS)
                consumed[pl.ds(row, ROWS), :] = sums[r] * xs[r]
            return 0

        lax.fori_loop(0, block // GROUP, quarter, 0)

    start(0, low_half(me), low_half(me), to_h_up)
    start(3, high_half(me), high_half(me), to_h_dn)
    start(1, high_half(me), high_half(me), to_h_up)
    start(2, low_half(me), low_half(me), to_h_dn)
    y_send(0, h)

    for load in loads[1:]:
        load.wait()
    mass[...] = biomass[...].astype(jnp.float32)
    pad = jnp.zeros((LANES - strains, LANES), jnp.float32)
    cap_t = jnp.concatenate([capacity[...], pad], axis=0).T
    aff_t = jnp.concatenate([affinity[...], pad], axis=0).T
    for s in range(strains):
        cap_rows[s] = jnp.broadcast_to(cap_t[:, s : s + 1], (LANES, LANES))
        aff_rows[s] = jnp.broadcast_to(aff_t[:, s : s + 1], (LANES, LANES))
    sec = jnp.concatenate([secretion[...].astype(jnp.float32), pad], axis=0).T
    sec = sec[:, :strains].astype(jnp.bfloat16)
    flux[...] = jnp.zeros_like(flux)
    gain[...] = jnp.zeros_like(gain)

    compute(me)
    y_pass(0, h)
    compute(at(y_dn, h))
    compute(at(y_up, h))
    y_last(0, h)
    compute(at(y_op, h))
    arrived(0, low_half(at(y, h_dn)))
    start(22, low_half(at(y, h_dn)), low_half(at(y, h_dn)), to_h_up)
    arrived(3, high_half(at(y, h_up)))
    start(23, high_half(at(y, h_up)), high_half(at(y, h_up)), to_h_dn)
    arrived(1, high_half(at(y, h_dn)))
    y_send(1, h_dn)
    arrived(2, low_half(at(y, h_up)))
    y_send(2, h_up)
    compute(at(y, h_dn))
    compute(at(y, h_up))
    y_pass(1, h_dn)
    y_pass(2, h_up)
    compute(at(y_dn, h_dn))
    compute(at(y_up, h_dn))
    compute(at(y_dn, h_up))
    compute(at(y_up, h_up))
    arrived(22, low_half(at(y, h_op)))
    part = low_half(at(y, h_op))
    start(16, part, part, to_y_up)
    start(17, part, part, to_y_dn)
    arrived(23, high_half(at(y, h_op)))
    part = high_half(at(y, h_op))
    start(18, part, part, to_y_up)
    start(19, part, part, to_y_dn)
    y_last(1, h_dn)
    y_last(2, h_up)
    compute(at(y_op, h_dn))
    compute(at(y_op, h_up))
    compute(at(y, h_op))
    arrived(16, low_half(at(y_dn, h_op)))
    start(20, low_half(at(y_dn, h_op)), low_half(at(y_dn, h_op)), to_y_up)
    arrived(19, high_half(at(y_up, h_op)))
    start(21, high_half(at(y_up, h_op)), high_half(at(y_up, h_op)), to_y_dn)
    start(24, biomass, halo_b.at[0], to_next)
    start(25, biomass, halo_b.at[1], to_prev)
    start(26, resources, halo_r.at[0], to_next)
    start(27, resources, halo_r.at[1], to_prev)
    arrived(18, high_half(at(y_dn, h_op)))
    compute(at(y_dn, h_op))
    arrived(17, low_half(at(y_up, h_op)))
    compute(at(y_up, h_op))
    arrived(20, low_half(at(y_op, h_op)))
    arrived(21, high_half(at(y_op, h_op)))
    compute(at(y_op, h_op))

    def to_product(s, _):
        value = (mass[s] * flux[s]).astype(jnp.bfloat16).astype(jnp.float32)
        product[pl.ds(pl.multiple_of(s * ROWS, ROWS), ROWS), :] = value
        return 0

    lax.fori_loop(0, strains, to_product, 0, unroll=4)

    rows = ROWS // PARTS
    first = rows // 2
    base = 28
    span = RING * block

    def lows(p):
        return range(p * rows, p * rows + first)

    def highs(p):
        return range(p * rows + first, (p + 1) * rows)

    def both(p):
        return range(p * rows, (p + 1) * rows)

    def of(rng):
        return pl.ds(rng.start, len(rng))

    def pairs_of(rng):
        return range(rng.start // 2, rng.stop // 2)

    def run(yy):
        return pl.ds(pl.multiple_of(yy * span, span), span)

    def pair(k, hh):
        at_h = pl.ds(pl.multiple_of(hh * block, block), block)
        return jnp.concatenate([reduced[2 * k, at_h], reduced[2 * k + 1, at_h]], axis=0)

    for p in range(PARTS):
        for q in both(p):
            made = product[pl.ds(q, strains, stride=ROWS), :].astype(jnp.bfloat16)
            secreted = jnp.dot(sec, made, preferred_element_type=jnp.float32)
            used = consumed[pl.ds(q, blocks * block, stride=ROWS), :]
            net[q] = secreted - used
            pass_y[q] = encode(net[q, run(y_op)])
        k = base + 8 * p
        start(k, pass_y.at[of(lows(p))], relay_y.at[of(lows(p))], to_y_up)
        start(k + 1, pass_y.at[of(highs(p))], relay_y.at[of(highs(p))], to_y_dn)

    for p in range(PARTS):
        k = base + 8 * p
        for q in highs(p):
            send_y[0, q] = encode(net[q, run(y_up)])
        for q in lows(p):
            send_y[1, q] = encode(net[q, run(y_dn)])
        arrived(k, relay_y.at[of(lows(p))])
        for q in lows(p):
            send_y[0, q] = encode(net[q, run(y_up)] + decode(relay_y[q]))
        start(k + 2, send_y.at[0, of(both(p))], sum_y.at[0, of(both(p))], to_y_up)
        arrived(k + 1, relay_y.at[of(highs(p))])
        for q in highs(p):
            send_y[1, q] = encode(net[q, run(y_dn)] + decode(relay_y[q]))
        start(k + 3, send_y.at[1, of(both(p))], sum_y.at[1, of(both(p))], to_y_dn)

    arrived(24, halo_b.at[0])
    arrived(25, halo_b.at[1])

    def update(s, _):
        m = mass[s]
        grown = gain[s] - maintenance[s]
        low = halo_b[0, s].astype(jnp.float32)
        high = halo_b[1, s].astype(jnp.float32)
        growth_out[s] = grown
        spread = motility[s] * laplace(m, low, high)
        biomass_out[s] = m + TIME_STEP * (m * grown + spread)
        return 0

    lax.fori_loop(0, strains, update, 0, unroll=2)
    stores = [
        pltpu.make_async_copy(growth_out, growth_hbm, store_sem.at[0]),
        pltpu.make_async_copy(biomass_out, biomass_hbm, store_sem.at[1]),
        pltpu.make_async_copy(resources_out, resources_hbm, store_sem.at[2]),
    ]
    stores[0].start()
    stores[1].start()

    for p in range(PARTS):
        k = base + 8 * p
        arrived(k + 2, sum_y.at[0, of(both(p))])
        arrived(k + 3, sum_y.at[1, of(both(p))])
        for q in both(p):
            others = decode(sum_y[0, q]) + decode(sum_y[1, q])
            reduced[q] = net[q, run(y)] + others
        for j in pairs_of(both(p)):
            pass_z[j] = encode(pair(j, h_op))
        low, high = of(pairs_of(lows(p))), of(pairs_of(highs(p)))
        start(k + 4, pass_z.at[low], relay_z.at[low], to_h_up)
        start(k + 5, pass_z.at[high], relay_z.at[high], to_h_dn)

    for p in range(PARTS):
        k = base + 8 * p
        low, high = pairs_of(lows(p)), pairs_of(highs(p))
        every = of(pairs_of(both(p)))
        for j in high:
            send_z[0, j] = encode(pair(j, h_up))
        for j in low:
            send_z[1, j] = encode(pair(j, h_dn))
        arrived(k + 4, relay_z.at[of(low)])
        for j in low:
            send_z[0, j] = encode(pair(j, h_up) + decode(relay_z[j]))
        start(k + 6, send_z.at[0, every], sum_z.at[0, every], to_h_up)
        arrived(k + 5, relay_z.at[of(high)])
        for j in high:
            send_z[1, j] = encode(pair(j, h_dn) + decode(relay_z[j]))
        start(k + 7, send_z.at[1, every], sum_z.at[1, every], to_h_dn)

    arrived(26, halo_r.at[0])
    arrived(27, halo_r.at[1])
    for r in range(block):
        value = resources[r]
        spread = diffusivity[r] * laplace(value, halo_r[0, r], halo_r[1, r])
        resources_out[r] = value + TIME_STEP * (spread + supply[r])
    for p in range(PARTS):
        k = base + 8 * p
        arrived(k + 6, sum_z.at[0, of(pairs_of(both(p)))])
        arrived(k + 7, sum_z.at[1, of(pairs_of(both(p)))])
        for j in pairs_of(both(p)):
            total = pair(j, h) + (decode(sum_z[0, j]) + decode(sum_z[1, j]))
            final[pl.ds(2 * j, block, stride=ROWS), :] = total[:block]
            final[pl.ds(2 * j + 1, block, stride=ROWS), :] = total[block:]
    for r in range(block):
        released = final[pl.ds(r * ROWS, ROWS), :]
        resources_out[r] = resources_out[r] + TIME_STEP * released
    stores[2].start()
    for c in started:
        c.wait_send()
    for store in stores:
        store.wait()


def store_kernel(a, b, c, a_out, b_out, c_out, a_mid, b_mid, c_mid, sem):
    chains = ((a, a_mid, a_out), (b, b_mid, b_out), (c, c_mid, c_out))
    loads = []
    stores = []
    for i, (src, mid, dst) in enumerate(chains):
        loads.append(pltpu.make_async_copy(src, mid, sem.at[0, i]))
        stores.append(pltpu.make_async_copy(mid, dst, sem.at[1, i]))
    for load in loads:
        load.start()
    for load, store in zip(loads, stores):
        load.wait()
        store.start()
    for store in stores:
        store.wait()


def per_device(
    biomass,
    resources,
    capacity,
    affinity,
    secretion,
    energy_yield,
    maintenance,
    motility,
    diffusivity,
    supply,
    n_space,
):
    strains, slab, plane = biomass.shape
    block = resources.shape[0]
    blocks = RING * RING
    tiles = plane // LANES

    def split(field):
        parts = field.reshape(field.shape[0], slab, tiles, LANES)
        return parts.transpose(0, 2, 1, 3).reshape(field.shape[0], ROWS, LANES)

    def join(field):
        parts = field.reshape(field.shape[0], tiles, slab, LANES)
        return parts.transpose(0, 2, 1, 3).reshape(field.shape[0], slab, plane)

    f32, bf16 = jnp.float32, jnp.bfloat16
    hbm = pl.BlockSpec(memory_space=pltpu.HBM)
    copies = 28 + 8 * PARTS
    outs = pl.pallas_call(
        functools.partial(kernel, n_space),
        out_shape=(
            jax.ShapeDtypeStruct((strains, ROWS, LANES), f32),
            jax.ShapeDtypeStruct((strains, ROWS, LANES), f32),
            jax.ShapeDtypeStruct((block, ROWS, LANES), f32),
        ),
        in_specs=[hbm] * 10,
        out_specs=(hbm,) * 3,
        scratch_shapes=[
            pltpu.VMEM((strains, ROWS, LANES), jnp.bfloat16),
            pltpu.VMEM((block, ROWS, LANES), f32),
            pltpu.VMEM(capacity.shape, f32),
            pltpu.VMEM(affinity.shape, f32),
            pltpu.VMEM((strains, blocks * block), jnp.bfloat16),
            pltpu.SMEM(energy_yield.shape, f32),
            pltpu.SMEM(maintenance.shape, f32),
            pltpu.SMEM(motility.shape, f32),
            pltpu.SMEM(diffusivity.shape, f32),
            pltpu.SMEM(supply.shape, f32),
            pltpu.VMEM((blocks, block, ROWS, LANES), jnp.bfloat16),
            pltpu.VMEM((strains, ROWS, LANES), f32),
            pltpu.VMEM((strains, LANES, LANES), f32),
            pltpu.VMEM((strains, LANES, LANES), f32),
            pltpu.VMEM((strains, ROWS, LANES), f32),
            pltpu.VMEM((strains, ROWS, LANES), f32),
            pltpu.VMEM((blocks * block * ROWS, LANES), f32),
            pltpu.VMEM((strains * ROWS, LANES), f32),
            pltpu.VMEM((ROWS, blocks * block, LANES), f32),
            pltpu.VMEM((ROWS, RING * block, LANES), bf16),
            pltpu.VMEM((ROWS, RING * block, LANES), bf16),
            pltpu.VMEM((2, ROWS, RING * block, LANES), bf16),
            pltpu.VMEM((2, ROWS, RING * block, LANES), bf16),
            pltpu.VMEM((ROWS, RING * block, LANES), f32),
            pltpu.VMEM((ROWS // 2, 2 * block, LANES), bf16),
            pltpu.VMEM((ROWS // 2, 2 * block, LANES), bf16),
            pltpu.VMEM((2, ROWS // 2, 2 * block, LANES), bf16),
            pltpu.VMEM((2, ROWS // 2, 2 * block, LANES), bf16),
            pltpu.VMEM((block * ROWS, LANES), f32),
            pltpu.VMEM((2, strains, ROWS, LANES), jnp.bfloat16),
            pltpu.VMEM((2, block, ROWS, LANES), f32),
            pltpu.SemaphoreType.DMA((copies,)),
            pltpu.SemaphoreType.DMA((copies,)),
            pltpu.SemaphoreType.DMA((10,)),
            pltpu.SemaphoreType.DMA((3,)),
            pltpu.VMEM((strains, ROWS, LANES), f32),
            pltpu.VMEM((strains, ROWS, LANES), f32),
            pltpu.VMEM((block, ROWS, LANES), f32),
        ],
        compiler_params=pltpu.CompilerParams(
            collective_id=0, has_side_effects=True, vmem_limit_bytes=67043328
        ),
    )(
        split(biomass),
        split(resources),
        capacity,
        affinity,
        secretion.T,
        energy_yield,
        maintenance,
        motility,
        diffusivity,
        supply,
    )
    outs = pl.pallas_call(
        store_kernel,
        out_shape=tuple(jax.ShapeDtypeStruct(out.shape, f32) for out in outs),
        in_specs=[hbm] * 3,
        out_specs=(hbm,) * 3,
        scratch_shapes=[
            *(pltpu.VMEM(out.shape, f32) for out in outs),
            pltpu.SemaphoreType.DMA((2, 3)),
        ],
        compiler_params=pltpu.CompilerParams(vmem_limit_bytes=67043328),
    )(*outs)
    return tuple(join(out) for out in outs)


def solution(mesh):
    return jax.shard_map(
        functools.partial(per_device, n_space=mesh.shape["space"]),
        mesh=mesh,
        in_specs=(
            P("species", "space", None),
            P("species", "space", None),
            P("species", None),
            P("species", None),
            P(None, "species"),
            P(),
            P("species"),
            P("species"),
            P("species"),
            P("species"),
        ),
        out_specs=(
            P("species", "space", None),
            P("species", "space", None),
            P("species", "space", None),
        ),
        check_vma=False,
    )
```

time: 67.6 us -> 56.2 us (0.83)
  local copies, waits for them, and re-layouts: 6.59 us -> 0 us
  Pallas kernels: 59.9 us -> 55.3 us
    unnamed x23 -> x0, local copies, waits for them, and re-layouts: 6.59 us -> none
    pallas_call x1, Pallas kernels: 59.9 us -> 53.5 us  [per_device(): pl.pallas_call(functools.partial(kernel, n_space), out_shape=(jax.ShapeDt...]
    pallas_call x0 -> x1, Pallas kernels: none -> 1.8 us  [per_device(): pl.pallas_call(store_kernel, out_shape=tuple((jax.ShapeDtypeStruct(out.sh...]
where the time goes in v2:
time: 56.2 us; the launch traced here: 55.9 us
  Pallas kernels  55.3 us (98%)
  between operations  0.64 us (1%)
    pallas_call x1, Pallas kernels, per_device(): pl.pallas_call(functools.partial(kernel, n_space), out_shape=(jax.ShapeDt...  53.5 us
    pallas_call x1, Pallas kernels, per_device(): pl.pallas_call(store_kernel, out_shape=tuple((jax.ShapeDtypeStruct(out.sh...  1.8 us

profile of v2, /device:TPU:6, one launch (start us, length us, event | category | flops | bytes accessed | tf_op | source)
XLA Modules:
  0.0 55.9 jit_solution(14034937432446506208)
XLA Ops:
  0.6 53.5 %shard_map.121 = (f32[32,16,128]{2,1,0:T(8,128)}, f32[32,16,128]{2,1,0:T(8,128)}, f32[8,16,128]{2,1,0:T(8,128)}) custom-call(bf16[32,16,128]{2,1,0:T(8,128)(2,1)} %bitcast.26, f32[8,16,128]{2,1,0:T(8,128)} %bitcast.27, f32[32,128]{1,0:T(8,128)} %capacity_in.1, f32[32,128]{1,0:T(8,128)} %affinity_in.1, bf16[32,128]{1,0:T(8,128)(2,1)} %bitcast.28, ...), custom_call_target="tpu_custom_call" | custom-call | tf_op jit(solution)/shard_map/pallas_call | solution.py:484
  54.1 1.8 %shard_map.122 = (f32[32,16,128]{2,1,0:T(8,128)}, f32[32,16,128]{2,1,0:T(8,128)}, f32[8,16,128]{2,1,0:T(8,128)}) custom-call(f32[32,16,128]{2,1,0:T(8,128)} %get-tuple-element.9.a, f32[32,16,128]{2,1,0:T(8,128)} %get-tuple-element.10.b, f32[8,16,128]{2,1,0:T(8,128)} %get-tuple-element.11.c), custom_call_target="tpu_custom_call" | custom-call | tf_op jit(solution)/shard_map/pallas_call | solution.py:548

commit v3 on v2

--- a/solution.py
+++ b/solution.py
@@ -10,8 +10,8 @@
 MESH = pl.DeviceIdType.MESH
 RING = 4
 GROUP = 4
-UNROLL = 8
-PARTS = 4
+UNROLL = 16
+PARTS = 2
 TIME_STEP = 0.25
 SMALL = 2.0**-6
 STEPS = 19.5
@@ -83,13 +83,9 @@
     consumed,
     product,
     net,
-    pass_y,
-    relay_y,
     send_y,
     sum_y,
     reduced,
-    pass_z,
-    relay_z,
     send_z,
     sum_z,
     final,
@@ -114,13 +110,15 @@
     h_up, h_dn, h_op = (lax.rem(h + k, RING) for k in (1, 3, 2))
     to_y_up = {"species": y_up * RING + h}
     to_y_dn = {"species": y_dn * RING + h}
+    to_y_op = {"species": y_op * RING + h}
     to_h_up = {"species": y * RING + h_up}
     to_h_dn = {"species": y * RING + h_dn}
+    to_h_op = {"species": y * RING + h_op}
     to_next = {"space": lax.rem(place + 1, n_space)}
     to_prev = {"space": lax.rem(place + n_space - 1, n_space)}
 
     barrier = pltpu.get_barrier_semaphore()
-    for target in (to_h_up, to_h_dn, to_y_up, to_y_dn, to_next, to_prev):
+    for target in (to_h_up, to_h_dn, to_y_up, to_y_dn, to_y_op, to_next, to_prev):
         pl.semaphore_signal(barrier, inc=1, device_id=target, device_id_type=MESH)
 
     pairs = (
@@ -144,7 +142,7 @@
     loads[0].wait()
     seen[me] = resources[...].astype(jnp.bfloat16)
 
-    pl.semaphore_wait(barrier, 6)
+    pl.semaphore_wait(barrier, 7)
 
     started = []
 
@@ -178,21 +176,19 @@
     def at(yy, hh):
         return yy * RING + hh
 
-    def y_send(column, hh):
-        start(4 + 4 * column, whole(at(y, hh)), whole(at(y, hh)), to_y_up)
-        start(5 + 4 * column, whole(at(y, hh)), whole(at(y, hh)), to_y_dn)
-
-    def y_pass(column, hh):
-        arrived(4 + 4 * column, whole(at(y_dn, hh)))
-        part = low_half(at(y_dn, hh))
-        start(6 + 4 * column, part, part, to_y_up)
-        arrived(5 + 4 * column, whole(at(y_up, hh)))
-        part = high_half(at(y_up, hh))
-        start(7 + 4 * column, part, part, to_y_dn)
-
-    def y_last(column, hh):
-        arrived(6 + 4 * column, low_half(at(y_op, hh)))
-        arrived(7 + 4 * column, high_half(at(y_op, hh)))
+    def y_send(column, part):
+        start(6 + 3 * column, part, part, to_y_up)
+        start(7 + 3 * column, part, part, to_y_dn)
+        start(8 + 3 * column, part, part, to_y_op)
+
+    def from_dn(column, part):
+        arrived(6 + 3 * column, part)
+
+    def from_up(column, part):
+        arrived(7 + 3 * column, part)
+
+    def from_op(column, part):
+        arrived(8 + 3 * column, part)
 
     def compute(b):
         def quarter(part, _):
@@ -233,7 +229,7 @@
     start(3, high_half(me), high_half(me), to_h_dn)
     start(1, high_half(me), high_half(me), to_h_up)
     start(2, low_half(me), low_half(me), to_h_dn)
-    y_send(0, h)
+    y_send(0, whole(me))
 
     for load in loads[1:]:
         load.wait()
@@ -250,54 +246,51 @@
     gain[...] = jnp.zeros_like(gain)
 
     compute(me)
-    y_pass(0, h)
+    from_dn(0, whole(at(y_dn, h)))
     compute(at(y_dn, h))
+    from_up(0, whole(at(y_up, h)))
     compute(at(y_up, h))
-    y_last(0, h)
+    arrived(0, low_half(at(y, h_dn)))
+    start(4, low_half(at(y, h_dn)), low_half(at(y, h_dn)), to_h_up)
+    arrived(3, high_half(at(y, h_up)))
+    start(5, high_half(at(y, h_up)), high_half(at(y, h_up)), to_h_dn)
+    arrived(1, high_half(at(y, h_dn)))
+    y_send(1, whole(at(y, h_dn)))
+    arrived(2, low_half(at(y, h_up)))
+    y_send(2, whole(at(y, h_up)))
+    from_op(0, whole(at(y_op, h)))
     compute(at(y_op, h))
-    arrived(0, low_half(at(y, h_dn)))
-    start(22, low_half(at(y, h_dn)), low_half(at(y, h_dn)), to_h_up)
-    arrived(3, high_half(at(y, h_up)))
-    start(23, high_half(at(y, h_up)), high_half(at(y, h_up)), to_h_dn)
-    arrived(1, high_half(at(y, h_dn)))
-    y_send(1, h_dn)
-    arrived(2, low_half(at(y, h_up)))
-    y_send(2, h_up)
     compute(at(y, h_dn))
     compute(at(y, h_up))
-    y_pass(1, h_dn)
-    y_pass(2, h_up)
+    from_dn(1, whole(at(y_dn, h_dn)))
     compute(at(y_dn, h_dn))
+    from_up(1, whole(at(y_up, h_dn)))
     compute(at(y_up, h_dn))
+    from_dn(2, whole(at(y_dn, h_up)))
     compute(at(y_dn, h_up))
+    arrived(4, low_half(at(y, h_op)))
+    y_send(3, low_half(at(y, h_op)))
+    arrived(5, high_half(at(y, h_op)))
+    y_send(4, high_half(at(y, h_op)))
+    from_up(2, whole(at(y_up, h_up)))
     compute(at(y_up, h_up))
-    arrived(22, low_half(at(y, h_op)))
-    part = low_half(at(y, h_op))
-    start(16, part, part, to_y_up)
-    start(17, part, part, to_y_dn)
-    arrived(23, high_half(at(y, h_op)))
-    part = high_half(at(y, h_op))
-    start(18, part, part, to_y_up)
-    start(19, part, part, to_y_dn)
-    y_last(1, h_dn)
-    y_last(2, h_up)
+    from_op(1, whole(at(y_op, h_dn)))
     compute(at(y_op, h_dn))
+    from_op(2, whole(at(y_op, h_up)))
     compute(at(y_op, h_up))
     compute(at(y, h_op))
-    arrived(16, low_half(at(y_dn, h_op)))
-    start(20, low_half(at(y_dn, h_op)), low_half(at(y_dn, h_op)), to_y_up)
-    arrived(19, high_half(at(y_up, h_op)))
-    start(21, high_half(at(y_up, h_op)), high_half(at(y_up, h_op)), to_y_dn)
-    start(24, biomass, halo_b.at[0], to_next)
-    start(25, biomass, halo_b.at[1], to_prev)
-    start(26, resources, halo_r.at[0], to_next)
-    start(27, resources, halo_r.at[1], to_prev)
-    arrived(18, high_half(at(y_dn, h_op)))
+    start(21, biomass, halo_b.at[0], to_next)
+    start(22, biomass, halo_b.at[1], to_prev)
+    start(23, resources, halo_r.at[0], to_next)
+    start(24, resources, halo_r.at[1], to_prev)
+    from_dn(3, low_half(at(y_dn, h_op)))
+    from_dn(4, high_half(at(y_dn, h_op)))
     compute(at(y_dn, h_op))
-    arrived(17, low_half(at(y_up, h_op)))
+    from_up(3, low_half(at(y_up, h_op)))
+    from_up(4, high_half(at(y_up, h_op)))
     compute(at(y_up, h_op))
-    arrived(20, low_half(at(y_op, h_op)))
-    arrived(21, high_half(at(y_op, h_op)))
+    from_op(3, low_half(at(y_op, h_op)))
+    from_op(4, high_half(at(y_op, h_op)))
     compute(at(y_op, h_op))
 
     def to_product(s, _):
@@ -308,24 +301,16 @@
     lax.fori_loop(0, strains, to_product, 0, unroll=4)
 
     rows = ROWS // PARTS
-    first = rows // 2
-    base = 28
+    base = 25
     span = RING * block
-
-    def lows(p):
-        return range(p * rows, p * rows + first)
-
-    def highs(p):
-        return range(p * rows + first, (p + 1) * rows)
-
-    def both(p):
-        return range(p * rows, (p + 1) * rows)
-
-    def of(rng):
-        return pl.ds(rng.start, len(rng))
-
-    def pairs_of(rng):
-        return range(rng.start // 2, rng.stop // 2)
+    y_others = ((y_op, to_y_op), (y_up, to_y_up), (y_dn, to_y_dn))
+    h_others = ((h_op, to_h_op), (h_up, to_h_up), (h_dn, to_h_dn))
+
+    def all_rows(p):
+        return pl.ds(p * rows, rows)
+
+    def all_pairs(p):
+        return pl.ds(p * rows // 2, rows // 2)
 
     def run(yy):
         return pl.ds(pl.multiple_of(yy * span, span), span)
@@ -335,33 +320,19 @@
         return jnp.concatenate([reduced[2 * k, at_h], reduced[2 * k + 1, at_h]], axis=0)
 
     for p in range(PARTS):
-        for q in both(p):
+        for q in range(p * rows, (p + 1) * rows):
             made = product[pl.ds(q, strains, stride=ROWS), :].astype(jnp.bfloat16)
             secreted = jnp.dot(sec, made, preferred_element_type=jnp.float32)
             used = consumed[pl.ds(q, blocks * block, stride=ROWS), :]
             net[q] = secreted - used
-            pass_y[q] = encode(net[q, run(y_op)])
-        k = base + 8 * p
-        start(k, pass_y.at[of(lows(p))], relay_y.at[of(lows(p))], to_y_up)
-        start(k + 1, pass_y.at[of(highs(p))], relay_y.at[of(highs(p))], to_y_dn)
-
-    for p in range(PARTS):
-        k = base + 8 * p
-        for q in highs(p):
-            send_y[0, q] = encode(net[q, run(y_up)])
-        for q in lows(p):
-            send_y[1, q] = encode(net[q, run(y_dn)])
-        arrived(k, relay_y.at[of(lows(p))])
-        for q in lows(p):
-            send_y[0, q] = encode(net[q, run(y_up)] + decode(relay_y[q]))
-        start(k + 2, send_y.at[0, of(both(p))], sum_y.at[0, of(both(p))], to_y_up)
-        arrived(k + 1, relay_y.at[of(highs(p))])
-        for q in highs(p):
-            send_y[1, q] = encode(net[q, run(y_dn)] + decode(relay_y[q]))
-        start(k + 3, send_y.at[1, of(both(p))], sum_y.at[1, of(both(p))], to_y_dn)
-
-    arrived(24, halo_b.at[0])
-    arrived(25, halo_b.at[1])
+            for i, (yy, _) in enumerate(y_others):
+                send_y[i, q] = encode(net[q, run(yy)])
+        for i, (_, target) in enumerate(y_others):
+            part = all_rows(p)
+            start(base + 6 * p + i, send_y.at[i, part], sum_y.at[i, part], target)
+
+    arrived(21, halo_b.at[0])
+    arrived(22, halo_b.at[1])
 
     def update(s, _):
         m = mass[s]
@@ -383,47 +354,29 @@
     stores[1].start()
 
     for p in range(PARTS):
-        k = base + 8 * p
-        arrived(k + 2, sum_y.at[0, of(both(p))])
-        arrived(k + 3, sum_y.at[1, of(both(p))])
-        for q in both(p):
-            others = decode(sum_y[0, q]) + decode(sum_y[1, q])
+        for i in range(3):
+            arrived(base + 6 * p + i, sum_y.at[i, all_rows(p)])
+        for q in range(p * rows, (p + 1) * rows):
+            others = decode(sum_y[0, q]) + decode(sum_y[1, q]) + decode(sum_y[2, q])
             reduced[q] = net[q, run(y)] + others
-        for j in pairs_of(both(p)):
-            pass_z[j] = encode(pair(j, h_op))
-        low, high = of(pairs_of(lows(p))), of(pairs_of(highs(p)))
-        start(k + 4, pass_z.at[low], relay_z.at[low], to_h_up)
-        start(k + 5, pass_z.at[high], relay_z.at[high], to_h_dn)
-
-    for p in range(PARTS):
-        k = base + 8 * p
-        low, high = pairs_of(lows(p)), pairs_of(highs(p))
-        every = of(pairs_of(both(p)))
-        for j in high:
-            send_z[0, j] = encode(pair(j, h_up))
-        for j in low:
-            send_z[1, j] = encode(pair(j, h_dn))
-        arrived(k + 4, relay_z.at[of(low)])
-        for j in low:
-            send_z[0, j] = encode(pair(j, h_up) + decode(relay_z[j]))
-        start(k + 6, send_z.at[0, every], sum_z.at[0, every], to_h_up)
-        arrived(k + 5, relay_z.at[of(high)])
-        for j in high:
-            send_z[1, j] = encode(pair(j, h_dn) + decode(relay_z[j]))
-        start(k + 7, send_z.at[1, every], sum_z.at[1, every], to_h_dn)
-
-    arrived(26, halo_r.at[0])
-    arrived(27, halo_r.at[1])
+        for i, (hh, target) in enumerate(h_others):
+            for j in range(p * rows // 2, (p + 1) * rows // 2):
+                send_z[i, j] = encode(pair(j, hh))
+            part = all_pairs(p)
+            start(base + 6 * p + 3 + i, send_z.at[i, part], sum_z.at[i, part], target)
+
+    arrived(23, halo_r.at[0])
+    arrived(24, halo_r.at[1])
     for r in range(block):
         value = resources[r]
         spread = diffusivity[r] * laplace(value, halo_r[0, r], halo_r[1, r])
         resources_out[r] = value + TIME_STEP * (spread + supply[r])
     for p in range(PARTS):
-        k = base + 8 * p
-        arrived(k + 6, sum_z.at[0, of(pairs_of(both(p)))])
-        arrived(k + 7, sum_z.at[1, of(pairs_of(both(p)))])
-        for j in pairs_of(both(p)):
-            total = pair(j, h) + (decode(sum_z[0, j]) + decode(sum_z[1, j]))
+        for i in range(3):
+            arrived(base + 6 * p + 3 + i, sum_z.at[i, all_pairs(p)])
+        for j in range(p * rows // 2, (p + 1) * rows // 2):
+            others = decode(sum_z[0, j]) + decode(sum_z[1, j]) + decode(sum_z[2, j])
+            total = pair(j, h) + others
             final[pl.ds(2 * j, block, stride=ROWS), :] = total[:block]
             final[pl.ds(2 * j + 1, block, stride=ROWS), :] = total[block:]
     for r in range(block):
@@ -480,7 +433,7 @@
 
     f32, bf16 = jnp.float32, jnp.bfloat16
     hbm = pl.BlockSpec(memory_space=pltpu.HBM)
-    copies = 28 + 8 * PARTS
+    copies = 25 + 6 * PARTS
     outs = pl.pallas_call(
         functools.partial(kernel, n_space),
         out_shape=(
@@ -510,15 +463,11 @@
             pltpu.VMEM((blocks * block * ROWS, LANES), f32),
             pltpu.VMEM((strains * ROWS, LANES), f32),
             pltpu.VMEM((ROWS, blocks * block, LANES), f32),
-            pltpu.VMEM((ROWS, RING * block, LANES), bf16),
-            pltpu.VMEM((ROWS, RING * block, LANES), bf16),
-            pltpu.VMEM((2, ROWS, RING * block, LANES), bf16),
-            pltpu.VMEM((2, ROWS, RING * block, LANES), bf16),
+            pltpu.VMEM((3, ROWS, RING * block, LANES), bf16),
+            pltpu.VMEM((3, ROWS, RING * block, LANES), bf16),
             pltpu.VMEM((ROWS, RING * block, LANES), f32),
-            pltpu.VMEM((ROWS // 2, 2 * block, LANES), bf16),
-            pltpu.VMEM((ROWS // 2, 2 * block, LANES), bf16),
-            pltpu.VMEM((2, ROWS // 2, 2 * block, LANES), bf16),
-            pltpu.VMEM((2, ROWS // 2, 2 * block, LANES), bf16),
+            pltpu.VMEM((3, ROWS // 2, 2 * block, LANES), bf16),
+            pltpu.VMEM((3, ROWS // 2, 2 * block, LANES), bf16),
             pltpu.VMEM((block * ROWS, LANES), f32),
             pltpu.VMEM((2, strains, ROWS, LANES), jnp.bfloat16),
             pltpu.VMEM((2, block, ROWS, LANES), f32),

time: 56.2 us -> 48.1 us (0.86)
  Pallas kernels: 55.3 us -> 47.3 us
    pallas_call x1, Pallas kernels: 53.5 us -> 45.5 us  [per_device(): pl.pallas_call(functools.partial(kernel, n_space), out_shape=(jax.ShapeDt...]
where the time goes in v3:
time: 48.1 us; the launch traced here: 47.9 us
  Pallas kernels  47.3 us (98%)
  between operations  0.64 us (1%)
    pallas_call x1, Pallas kernels, per_device(): pl.pallas_call(functools.partial(kernel, n_space), out_shape=(jax.ShapeDt...  45.5 us
    pallas_call x1, Pallas kernels, per_device(): pl.pallas_call(store_kernel, out_shape=tuple((jax.ShapeDtypeStruct(out.sh...  1.8 us

profile of v3, /device:TPU:6, one launch (start us, length us, event | category | flops | bytes accessed | tf_op | source)
XLA Modules:
  0.0 47.9 jit_solution(14586079059388902854)
XLA Ops:
  0.6 45.5 %shard_map.121 = (f32[32,16,128]{2,1,0:T(8,128)}, f32[32,16,128]{2,1,0:T(8,128)}, f32[8,16,128]{2,1,0:T(8,128)}) custom-call(bf16[32,16,128]{2,1,0:T(8,128)(2,1)} %bitcast.26, f32[8,16,128]{2,1,0:T(8,128)} %bitcast.27, f32[32,128]{1,0:T(8,128)} %capacity_in.1, f32[32,128]{1,0:T(8,128)} %affinity_in.1, bf16[32,128]{1,0:T(8,128)(2,1)} %bitcast.28, ...), custom_call_target="tpu_custom_call" | custom-call | tf_op jit(solution)/shard_map/pallas_call | solution.py:437
  46.1 1.8 %shard_map.122 = (f32[32,16,128]{2,1,0:T(8,128)}, f32[32,16,128]{2,1,0:T(8,128)}, f32[8,16,128]{2,1,0:T(8,128)}) custom-call(f32[32,16,128]{2,1,0:T(8,128)} %get-tuple-element.9.a, f32[32,16,128]{2,1,0:T(8,128)} %get-tuple-element.10.b, f32[8,16,128]{2,1,0:T(8,128)} %get-tuple-element.11.c), custom_call_target="tpu_custom_call" | custom-call | tf_op jit(solution)/shard_map/pallas_call | solution.py:497

commit v4 on v3

--- a/solution.py
+++ b/solution.py
@@ -11,7 +11,7 @@
 RING = 4
 GROUP = 4
 UNROLL = 16
-PARTS = 2
+PIECES = (8, 8)
 TIME_STEP = 0.25
 SMALL = 2.0**-6
 STEPS = 19.5
@@ -76,8 +76,8 @@
     supply,
     seen,
     mass,
-    cap_rows,
-    aff_rows,
+    shifts,
+    slopes,
     flux,
     gain,
     consumed,
@@ -193,7 +193,9 @@
     def compute(b):
         def quarter(part, _):
             first_r = part * GROUP
-            xs = [seen[b, first_r + r].astype(jnp.float32) for r in range(GROUP)]
+            inverse = [
+                1.0 / seen[b, first_r + r].astype(jnp.float32) for r in range(GROUP)
+            ]
             es = [energy_yield[b * block + first_r + r] for r in range(GROUP)]
 
             def strain(i, sums):
@@ -205,11 +207,10 @@
                     g = gain[s]
                     for r in range(GROUP):
                         row = pl.ds(b * block + first_r + r, 1)
-                        a = jnp.broadcast_to(aff_rows[s, row, :], (ROWS, LANES))
-                        c = jnp.broadcast_to(cap_rows[s, row, :], (ROWS, LANES))
-                        v = c / (a + xs[r])
-                        sums[r] = sums[r] + m * v
-                        u = xs[r] * v
+                        slope = jnp.broadcast_to(slopes[s, row, :], (ROWS, LANES))
+                        shift = jnp.broadcast_to(shifts[s, row, :], (ROWS, LANES))
+                        u = 1.0 / (slope * inverse[r] + shift)
+                        sums[r] = sums[r] + m * u
                         f = f + u
                         g = g + es[r] * u
                     flux[s] = f
@@ -220,7 +221,7 @@
             sums = lax.fori_loop(0, strains // UNROLL, strain, (zero,) * GROUP)
             for r in range(GROUP):
                 row = pl.multiple_of((b * block + first_r + r) * ROWS, ROWS)
-                consumed[pl.ds(row, ROWS), :] = sums[r] * xs[r]
+                consumed[pl.ds(row, ROWS), :] = sums[r]
             return 0
 
         lax.fori_loop(0, block // GROUP, quarter, 0)
@@ -235,11 +236,11 @@
         load.wait()
     mass[...] = biomass[...].astype(jnp.float32)
     pad = jnp.zeros((LANES - strains, LANES), jnp.float32)
-    cap_t = jnp.concatenate([capacity[...], pad], axis=0).T
-    aff_t = jnp.concatenate([affinity[...], pad], axis=0).T
+    shift_t = jnp.concatenate([1.0 / capacity[...], pad], axis=0).T
+    slope_t = jnp.concatenate([affinity[...] / capacity[...], pad], axis=0).T
     for s in range(strains):
-        cap_rows[s] = jnp.broadcast_to(cap_t[:, s : s + 1], (LANES, LANES))
-        aff_rows[s] = jnp.broadcast_to(aff_t[:, s : s + 1], (LANES, LANES))
+        shifts[s] = jnp.broadcast_to(shift_t[:, s : s + 1], (LANES, LANES))
+        slopes[s] = jnp.broadcast_to(slope_t[:, s : s + 1], (LANES, LANES))
     sec = jnp.concatenate([secretion[...].astype(jnp.float32), pad], axis=0).T
     sec = sec[:, :strains].astype(jnp.bfloat16)
     flux[...] = jnp.zeros_like(flux)
@@ -300,17 +301,17 @@
 
     lax.fori_loop(0, strains, to_product, 0, unroll=4)
 
-    rows = ROWS // PARTS
     base = 25
+    edges = [sum(PIECES[:p]) for p in range(len(PIECES) + 1)]
     span = RING * block
     y_others = ((y_op, to_y_op), (y_up, to_y_up), (y_dn, to_y_dn))
     h_others = ((h_op, to_h_op), (h_up, to_h_up), (h_dn, to_h_dn))
 
     def all_rows(p):
-        return pl.ds(p * rows, rows)
+        return pl.ds(edges[p], PIECES[p])
 
     def all_pairs(p):
-        return pl.ds(p * rows // 2, rows // 2)
+        return pl.ds(edges[p] // 2, PIECES[p] // 2)
 
     def run(yy):
         return pl.ds(pl.multiple_of(yy * span, span), span)
@@ -319,8 +320,8 @@
         at_h = pl.ds(pl.multiple_of(hh * block, block), block)
         return jnp.concatenate([reduced[2 * k, at_h], reduced[2 * k + 1, at_h]], axis=0)
 
-    for p in range(PARTS):
-        for q in range(p * rows, (p + 1) * rows):
+    for p in range(len(PIECES)):
+        for q in range(edges[p], edges[p + 1]):
             made = product[pl.ds(q, strains, stride=ROWS), :].astype(jnp.bfloat16)
             secreted = jnp.dot(sec, made, preferred_element_type=jnp.float32)
             used = consumed[pl.ds(q, blocks * block, stride=ROWS), :]
@@ -353,14 +354,14 @@
     stores[0].start()
     stores[1].start()
 
-    for p in range(PARTS):
+    for p in range(len(PIECES)):
         for i in range(3):
             arrived(base + 6 * p + i, sum_y.at[i, all_rows(p)])
-        for q in range(p * rows, (p + 1) * rows):
+        for q in range(edges[p], edges[p + 1]):
             others = decode(sum_y[0, q]) + decode(sum_y[1, q]) + decode(sum_y[2, q])
             reduced[q] = net[q, run(y)] + others
         for i, (hh, target) in enumerate(h_others):
-            for j in range(p * rows // 2, (p + 1) * rows // 2):
+            for j in range(edges[p] // 2, edges[p + 1] // 2):
                 send_z[i, j] = encode(pair(j, hh))
             part = all_pairs(p)
             start(base + 6 * p + 3 + i, send_z.at[i, part], sum_z.at[i, part], target)
@@ -371,10 +372,10 @@
         value = resources[r]
         spread = diffusivity[r] * laplace(value, halo_r[0, r], halo_r[1, r])
         resources_out[r] = value + TIME_STEP * (spread + supply[r])
-    for p in range(PARTS):
+    for p in range(len(PIECES)):
         for i in range(3):
             arrived(base + 6 * p + 3 + i, sum_z.at[i, all_pairs(p)])
-        for j in range(p * rows // 2, (p + 1) * rows // 2):
+        for j in range(edges[p] // 2, edges[p + 1] // 2):
             others = decode(sum_z[0, j]) + decode(sum_z[1, j]) + decode(sum_z[2, j])
             total = pair(j, h) + others
             final[pl.ds(2 * j, block, stride=ROWS), :] = total[:block]
@@ -433,7 +434,7 @@
 
     f32, bf16 = jnp.float32, jnp.bfloat16
     hbm = pl.BlockSpec(memory_space=pltpu.HBM)
-    copies = 25 + 6 * PARTS
+    copies = 25 + 6 * len(PIECES)
     outs = pl.pallas_call(
         functools.partial(kernel, n_space),
         out_shape=(

time: 48.1 us -> 47.5 us (0.988)
  Pallas kernels: 47.3 us -> 46.6 us
    pallas_call x1, Pallas kernels: 45.5 us -> 44.8 us  [per_device(): pl.pallas_call(functools.partial(kernel, n_space), out_shape=(jax.ShapeDt...]
where the time goes in v4:
time: 47.5 us; the launch traced here: 47.2 us
  Pallas kernels  46.6 us (98%)
  between operations  0.64 us (1%)
    pallas_call x1, Pallas kernels, per_device(): pl.pallas_call(functools.partial(kernel, n_space), out_shape=(jax.ShapeDt...  44.8 us
    pallas_call x1, Pallas kernels, per_device(): pl.pallas_call(store_kernel, out_shape=tuple((jax.ShapeDtypeStruct(out.sh...  1.8 us

profile of v4, /device:TPU:6, one launch (start us, length us, event | category | flops | bytes accessed | tf_op | source)
XLA Modules:
  0.0 47.2 jit_solution(14418079031419129391)
XLA Ops:
  0.6 44.8 %shard_map.121 = (f32[32,16,128]{2,1,0:T(8,128)}, f32[32,16,128]{2,1,0:T(8,128)}, f32[8,16,128]{2,1,0:T(8,128)}) custom-call(bf16[32,16,128]{2,1,0:T(8,128)(2,1)} %bitcast.26, f32[8,16,128]{2,1,0:T(8,128)} %bitcast.27, f32[32,128]{1,0:T(8,128)} %capacity_in.1, f32[32,128]{1,0:T(8,128)} %affinity_in.1, bf16[32,128]{1,0:T(8,128)(2,1)} %bitcast.28, ...), custom_call_target="tpu_custom_call" | custom-call | tf_op jit(solution)/shard_map/pallas_call | solution.py:438
  45.4 1.8 %shard_map.122 = (f32[32,16,128]{2,1,0:T(8,128)}, f32[32,16,128]{2,1,0:T(8,128)}, f32[8,16,128]{2,1,0:T(8,128)}) custom-call(f32[32,16,128]{2,1,0:T(8,128)} %get-tuple-element.9.a, f32[32,16,128]{2,1,0:T(8,128)} %get-tuple-element.10.b, f32[8,16,128]{2,1,0:T(8,128)} %get-tuple-element.11.c), custom_call_target="tpu_custom_call" | custom-call | tf_op jit(solution)/shard_map/pallas_call | solution.py:498
